TPU v7x, 256 devices: a whole 4x4x8 slice. The times are simulated.
256 devices in a mesh: dp: 8 (over x, z_hi), context: 32 (over y, z_lo, core).
Axes of the slice: x: 4, y: 4, z: 8 (z_hi: 2, z_lo: 4; z = z_hi * 4 + z_lo), core: 2. Of those that a mesh axis runs over, the one named last changes fastest.
Arguments:
- grad_out: bfloat16 [8, 4096, 4096], P('dp', 'context'), may hold values from -6 to 6
- attn: bfloat16 [8, 4096, 4096], P('dp', 'context'), may hold values from -0.032958984 to 0.032958984
- w_out: bfloat16 [4096, 4096], P('context'), may hold values from -0.09375 to 0.09375
Outputs:
- grad_attn: bfloat16 [8, 4096, 4096], P('dp', None, 'context')
- grad_w: bfloat16 [4096, 4096], P('context')
All inputs are finite; a program needn't handle non-finite values.
Results may differ from a plain program's by a relative error of at most 0.013.
Values may be sent and summed in bfloat16 or wider, within the bound.
No kernel may reach another device: no remote copies, remote signals or barrier semaphores. Data moves between devices by JAX's collectives and lax.ppermute only.
A program may use at most 128 MiB of HBM per device.

v0:
```python
import jax
import jax.numpy as jnp
from jax import lax
from jax.sharding import Mesh, PartitionSpec as P

CHUNKS = (2048, 2048)
RING8 = ("h", "l")


def shift(v, axis, by):
    n = lax.axis_size(axis)
    return lax.ppermute(v, axis, [(i, (i + by) % n) for i in range(n)])


def exchange(v, axis):
    return lax.all_to_all(v, axis, split_axis=0, concat_axis=0, tiled=True)


def after(v, *others):
    return lax.optimization_barrier((v, *others))[0]


def around(own, axis):
    half = own.shape[0] // 2
    above = shift(own, axis, -1)
    below = shift(own, axis, 1)
    far_a = shift(above[:half], axis, -1)
    far_b = shift(below[half:], axis, 1)
    return [own, above, far_a, far_b, below]


def local(grad_out, attn, w_out):
    f32, bf16 = (jnp.float32, jnp.bfloat16)
    g = grad_out[0]
    a = attn[0]
    toks, feats = g.shape
    heads = w_out.shape[0]
    quarter = heads // 4
    l = lax.axis_index("l")
    cuts, at = ([], 0)
    for size in CHUNKS:
        size = size * feats // sum(CHUNKS)
        cuts.append((at, at + size))
        at += size
    g_cols = [lax.all_gather(g[:, lo:hi], ("y", "c"), axis=0, tiled=True) for lo, hi in cuts]
    a = a.reshape(toks, 4, 4, 2, heads).transpose(1, 3, 0, 2, 4).reshape(8, toks, 4 * heads)
    acts = exchange(a, ("y", "c")).reshape(8 * toks, 4 * heads)
    w_parts = around(w_out, RING8)
    sums, part = ([], None)
    for gj in g_cols:
        if part is not None:
            gj = after(gj, part)
        part = lax.dot_general(
            acts, gj, (((0,), (0,)), ((), ())), preferred_element_type=f32
        ).astype(bf16)
        part = part.reshape(4, 4, quarter, -1)
        tot = exchange(part.transpose(1, 0, 2, 3), "x").astype(f32).sum(0).astype(bf16)
        tot = exchange(tot, "l").astype(f32).sum(0).astype(bf16)
        tot = (tot.astype(f32) + shift(tot, "h", 1).astype(f32)).astype(bf16)
        sums.append(exchange(jnp.broadcast_to(tot[None], (4,) + tot.shape), "x").reshape(heads, -1))
    grad_w = jnp.concatenate(sums, 1)
    w = jnp.concatenate(w_parts, 0)
    w = lax.dynamic_slice_in_dim(jnp.concatenate([w, w], 0), (4 - l & 3) * heads, 4 * heads, 0)
    gall = after(jnp.concatenate(g_cols, 1), part)
    res = lax.dot_general(gall, w, (((1,), (1,)), ((), ())), preferred_element_type=f32).astype(
        bf16
    )
    res = res.reshape(8 * toks, 4, heads).transpose(1, 0, 2)
    out = exchange(res, "l")
    out = out.reshape(4, 4, 2 * toks, heads).transpose(1, 0, 2, 3).reshape(1, 4 * 8 * toks, heads)
    return (out, grad_w)


def solution(mesh):
    fine = Mesh(mesh.devices.reshape(4, 2, 4, 4, 2), ("x", "h", "y", "l", "c"))
    dp, context = (("x", "h"), ("y", "l", "c"))
    in_specs = (P(dp, context, None), P(dp, context, None), P(context, None))
    out_specs = (P(dp, None, context), P(context, None))
    return jax.shard_map(local, mesh=fine, in_specs=in_specs, out_specs=out_specs, check_vma=False)
```

profile of v0, /device:TPU:2, one launch (start us, length us, event | category | flops | bytes accessed | tf_op | source)
XLA Modules:
  0.0 265.9 jit_solution(8318306603552850730)
XLA Ops:
  10.4 5.9 %collective-permute-start = (bf16[128,4096]{1,0:T(8,128)(2,1)}, bf16[128,4096]{1,0:T(8,128)(2,1)S(1)}, u32[]{:S(2)}, u32[]{:S(2)}) collective-permute-start(bf16[128,4096]{1,0:T(8,128)(2,1)} %param.5), channel_id=1, source_target_pairs={{0,38},{2,0},{4,2},{6,4},{32,6},{34,32},{36,34},{38,36},{1,39},{3,... | collective-permute-start | bytes 3145736 | tf_op jit(solution)/shard_map/ppermute | solution.py:12
  20.9 4.5 %all-to-all-start = ((bf16[8,128,512]{1,2,0:T(8,128)(2,1)}), bf16[8,128,512]{1,2,0:T(8,128)(2,1)}, u32[]{:S(2)}, u32[]{:S(2)}) async-start(bf16[8,128,512]{1,2,0:T(8,128)(2,1)} %bitcast.33), calls=%async_computation | async-start | bytes 2097152 | tf_op jit(solution)/shard_map/all_to_all | solution.py:16
  26.4 26.3 %all-to-all-done = bf16[8,128,512]{1,2,0:T(8,128)(2,1)} async-done(((bf16[8,128,512]{1,2,0:T(8,128)(2,1)}), bf16[8,128,512]{1,2,0:T(8,128)(2,1)}, u32[]{:S(2)}, u32[]{:S(2)}) %all-to-all-start) | async-done | bytes 1048608 | tf_op jit(solution)/shard_map/all_to_all | solution.py:16
  55.1 3.2 %collective-permute-start.1 = (bf16[64,4096]{1,0:T(8,128)(2,1)}, bf16[64,4096]{1,0:T(8,128)(2,1)}, u32[]{:S(2)}, u32[]{:S(2)}) collective-permute-start(bf16[64,4096]{1,0:T(8,128)(2,1)} %slice.18), channel_id=1, source_target_pairs={{0,38},{2,0},{4,2},{6,4},{32,6},{34,32},{36,34},{38,36},{1,39},{3,... | collective-permute-start | bytes 1572872 | tf_op jit(solution)/shard_map/ppermute | solution.py:12
  59.1 5.9 %convolution_convert_fusion.1 = bf16[512,2048]{1,0:T(8,128)(2,1)} fusion(bf16[1024,512]{1,0:T(8,128)(2,1)S(1)} %bitcast.40, bf16[1024,2048]{1,0:T(8,128)(2,1)} %all-gather.3.cloned.1.call-done), kind=kOutput, calls=%fused_computation.4 | convolution fusion | flops 2148532224 | bytes 7340032 | tf_op jit(solution)/shard_map/dot_general | solution.py:53
  65.0 28.4 %all-gather.5.cloned.1.call-done = bf16[1024,2048]{1,0:T(8,128)(2,1)} async-done(((bf16[128,2048]{1,0:T(8,128)(2,1)}), bf16[1024,2048]{1,0:T(8,128)(2,1)}) %all-gather.5.cloned.1.call-update) | async-done | bytes 4194320 | tf_op jit(solution)/shard_map/all_gather | solution.py:45
  93.4 4.6 %convolution_convert_fusion = bf16[2048,512]{0,1:T(8,128)(2,1)S(1)} fusion(bf16[1024,2048]{1,0:T(8,128)(2,1)} %all-gather.5.cloned.1.call-done, bf16[1024,512]{1,0:T(8,128)(2,1)S(1)} %bitcast.41), kind=kOutput, calls=%fused_computation.3 | convolution fusion | flops 2148532224 | bytes 7340032 | tf_op jit(solution)/shard_map/dot_general | solution.py:53
  99.6 4.8 %all-to-all-start.5 = ((bf16[4,4,32,2048]{3,2,1,0:T(8,128)(2,1)}), bf16[4,4,32,2048]{3,2,1,0:T(8,128)(2,1)S(1)}, u32[]{:S(2)}, u32[]{:S(2)}) async-start(bf16[4,4,32,2048]{3,2,1,0:T(8,128)(2,1)} %bitcast.31), calls=%async_computation.5 | async-start | bytes 4194304 | tf_op jit(solution)/shard_map/all_to_all | solution.py:16
  111.5 3.2 %copy.26 = bf16[4,4,32,2048]{3,2,0,1:T(8,128)(2,1)} copy(bf16[4,4,32,2048]{3,2,1,0:T(8,128)(2,1)} %bitcast.35) | data formatting | bytes 4194304 | tf_op jit(solution)/shard_map/reshape | solution.py:56
  114.8 14.9 %all-to-all-done.5 = bf16[4,4,32,2048]{3,2,1,0:T(8,128)(2,1)S(1)} async-done(((bf16[4,4,32,2048]{3,2,1,0:T(8,128)(2,1)}), bf16[4,4,32,2048]{3,2,1,0:T(8,128)(2,1)S(1)}, u32[]{:S(2)}, u32[]{:S(2)}) %all-to-all-start.5) | async-done | bytes 2097184 | tf_op jit(solution)/shard_map/all_to_all | solution.py:16
  129.7 5.9 %all-to-all-start.2 = ((bf16[4,4,32,2048]{3,2,1,0:T(8,128)(2,1)}), bf16[4,4,32,2048]{3,2,1,0:T(8,128)(2,1)}, u32[]{:S(2)}, u32[]{:S(2)}) async-start(bf16[4,4,32,2048]{3,2,1,0:T(8,128)(2,1)} %bitcast.32), calls=%async_computation.2 | async-start | bytes 4194304 | tf_op jit(solution)/shard_map/all_to_all | solution.py:16
  145.3 14.9 %all-to-all-done.2 = bf16[4,4,32,2048]{3,2,1,0:T(8,128)(2,1)} async-done(((bf16[4,4,32,2048]{3,2,1,0:T(8,128)(2,1)}), bf16[4,4,32,2048]{3,2,1,0:T(8,128)(2,1)}, u32[]{:S(2)}, u32[]{:S(2)}) %all-to-all-start.2) | async-done | bytes 2097184 | tf_op jit(solution)/shard_map/all_to_all | solution.py:16
  160.1 4.8 %all-to-all-start.6 = ((bf16[4,32,2048]{2,1,0:T(8,128)(2,1)}), bf16[4,32,2048]{2,1,0:T(8,128)(2,1)S(1)}, u32[]{:S(2)}, u32[]{:S(2)}) async-start(bf16[4,32,2048]{2,1,0:T(8,128)(2,1)} %reduce_sum.50), calls=%async_computation.6 | async-start | bytes 1048576 | tf_op jit(solution)/shard_map/all_to_all | solution.py:16
  166.1 7.8 %pad_maximum_fusion = bf16[1024,4096]{1,0:T(8,128)(2,1)} fusion(bf16[1024,2048]{1,0:T(8,128)(2,1)} %all-gather.5.cloned.1.call-done, bf16[1024,2048]{1,0:T(8,128)(2,1)} %all-gather.3.cloned.1.call-done), kind=kLoop, calls=%fused_computation | loop fusion | flops 16777216 | bytes 16777216 | tf_op jit(solution)/shard_map/concatenate | solution.py:64
  177.8 4.1 %all-to-all-start.3 = ((bf16[4,32,2048]{2,1,0:T(8,128)(2,1)}), bf16[4,32,2048]{2,1,0:T(8,128)(2,1)S(1)}, u32[]{:S(2)}, u32[]{:S(2)}) async-start(bf16[4,32,2048]{2,1,0:T(8,128)(2,1)} %reduce_sum.48), calls=%async_computation.3 | async-start | bytes 1048576 | tf_op jit(solution)/shard_map/all_to_all | solution.py:16
  181.9 10.1 %fusion.2 = bf16[1024,512]{0,1:T(8,128)(2,1)} fusion(bf16[1024,4096]{1,0:T(8,128)(2,1)} %pad_maximum_fusion, bf16[1024,4096]{1,0:T(8,128)(2,1)} %constant_dynamic-update-slice_fusion, s32[]{:T(128)S(6)} %select_n.3), kind=kOutput, calls=%fused_computation.7 | convolution fusion | flops 4295491584 | bytes 13631492 | tf_op jit(solution)/shard_map/dot_general | solution.py:65
  194.2 3.5 %all-to-all-start.1 = ((bf16[4,1024,128]{1,2,0:T(8,128)(2,1)}), bf16[4,1024,128]{1,2,0:T(8,128)(2,1)S(1)}, u32[]{:S(2)}, u32[]{:S(2)}) async-start(bf16[4,1024,128]{1,2,0:T(8,128)(2,1)} %bitcast.9), calls=%async_computation.1 | async-start | bytes 2097152 | tf_op jit(solution)/shard_map/all_to_all | solution.py:16
  197.8 5.1 %collective-permute-start.5 = (bf16[32,2048]{1,0:T(8,128)(2,1)S(1)}, bf16[32,2048]{1,0:T(8,128)(2,1)S(1)}, u32[]{:S(2)}, u32[]{:S(2)}) collective-permute-start(bf16[32,2048]{1,0:T(8,128)(2,1)S(1)} %reduce_sum.51), channel_id=1, source_target_pairs={{0,32},{32,0},{1,33},{33,1},{2,34},{34,2},{3,35},{35,3},{4,36},{36... | collective-permute-start | bytes 393224 | tf_op jit(solution)/shard_map/ppermute | solution.py:12
  204.0 24.7 %collective-permute-done.5 = bf16[32,2048]{1,0:T(8,128)(2,1)S(1)} collective-permute-done((bf16[32,2048]{1,0:T(8,128)(2,1)S(1)}, bf16[32,2048]{1,0:T(8,128)(2,1)S(1)}, u32[]{:S(2)}, u32[]{:S(2)}) %collective-permute-start.5) | collective-permute-done | bytes 131104 | tf_op jit(solution)/shard_map/ppermute | solution.py:12
  228.7 3.7 %all-to-all-done.1 = bf16[4,1024,128]{1,2,0:T(8,128)(2,1)S(1)} async-done(((bf16[4,1024,128]{1,2,0:T(8,128)(2,1)}), bf16[4,1024,128]{1,2,0:T(8,128)(2,1)S(1)}, u32[]{:S(2)}, u32[]{:S(2)}) %all-to-all-start.1) | async-done | bytes 1048608 | tf_op jit(solution)/shard_map/all_to_all | solution.py:16
  233.2 4.9 %all-to-all-start.7 = ((bf16[4,32,2048]{2,1,0:T(8,128)(2,1)}), bf16[4,32,2048]{2,1,0:T(8,128)(2,1)S(1)}, u32[]{:S(2)}, u32[]{:S(2)}) async-start(bf16[4,32,2048]{2,1,0:T(8,128)(2,1)} %broadcast_in_dim.5), calls=%async_computation.7 | async-start | bytes 1048576 | tf_op jit(solution)/shard_map/all_to_all | solution.py:16
  238.2 7.5 %all-to-all-done.7 = bf16[4,32,2048]{2,1,0:T(8,128)(2,1)S(1)} async-done(((bf16[4,32,2048]{2,1,0:T(8,128)(2,1)}), bf16[4,32,2048]{2,1,0:T(8,128)(2,1)S(1)}, u32[]{:S(2)}, u32[]{:S(2)}) %all-to-all-start.7) | async-done | bytes 524320 | tf_op jit(solution)/shard_map/all_to_all | solution.py:16
  246.5 4.9 %all-to-all-start.4 = ((bf16[4,32,2048]{2,1,0:T(8,128)(2,1)}), bf16[4,32,2048]{2,1,0:T(8,128)(2,1)S(1)}, u32[]{:S(2)}, u32[]{:S(2)}) async-start(bf16[4,32,2048]{2,1,0:T(8,128)(2,1)} %broadcast_in_dim.4), calls=%async_computation.4 | async-start | bytes 1048576 | tf_op jit(solution)/shard_map/all_to_all | solution.py:16
  253.6 4.4 %all-to-all-done.4 = bf16[4,32,2048]{2,1,0:T(8,128)(2,1)S(1)} async-done(((bf16[4,32,2048]{2,1,0:T(8,128)(2,1)}), bf16[4,32,2048]{2,1,0:T(8,128)(2,1)S(1)}, u32[]{:S(2)}, u32[]{:S(2)}) %all-to-all-start.4) | async-done | bytes 524320 | tf_op jit(solution)/shard_map/all_to_all | solution.py:16
  (47 shorter events, 43.9 us)
Async XLA Ops:
  7.2 18.2 %copy-start.1 = (bf16[128,4096]{1,0:T(8,128)(2,1)S(1)}, bf16[128,4096]{1,0:T(8,128)(2,1)}, u32[]{:S(2)}) copy-start(bf16[128,4096]{1,0:T(8,128)(2,1)} %param.5) | copy-start | bytes 3145732
  7.2 51.9 %all-gather.3.cloned.1.call-start = ((), (), s32[]{:S(2)}) async-start(), calls=%async_computation.8 | async-start | bytes 4718592 | tf_op jit(solution)/shard_map/all_gather | solution.py:45
  9.6 83.8 %all-gather.5.cloned.1.call-start = ((), (), s32[]{:S(2)}) async-start(), calls=%async_computation.9 | async-start | bytes 4718592 | tf_op jit(solution)/shard_map/all_gather | solution.py:45
  10.4 43.8 %collective-permute-start = (bf16[128,4096]{1,0:T(8,128)(2,1)}, bf16[128,4096]{1,0:T(8,128)(2,1)S(1)}, u32[]{:S(2)}, u32[]{:S(2)}) collective-permute-start(bf16[128,4096]{1,0:T(8,128)(2,1)} %param.5), channel_id=1, source_target_pairs={{0,38},{2,0},{4,2},{6,4},{32,6},{34,32},{36,34},{38,36},{1,39},{3,... | collective-permute-start | bytes 3145736 | tf_op jit(solution)/shard_map/ppermute | solution.py:12
  16.3 42.0 %collective-permute-start.2 = (bf16[128,4096]{1,0:T(8,128)(2,1)}, bf16[128,4096]{1,0:T(8,128)(2,1)S(1)}, u32[]{:S(2)}, u32[]{:S(2)}) collective-permute-start(bf16[128,4096]{1,0:T(8,128)(2,1)} %param.5), channel_id=1, source_target_pairs={{0,2},{2,4},{4,6},{6,32},{32,34},{34,36},{36,38},{38,0},{1,3},{3,5... | collective-permute-start | bytes 3145736 | tf_op jit(solution)/shard_map/ppermute | solution.py:12
  20.9 31.8 %all-to-all-start = ((bf16[8,128,512]{1,2,0:T(8,128)(2,1)}), bf16[8,128,512]{1,2,0:T(8,128)(2,1)}, u32[]{:S(2)}, u32[]{:S(2)}) async-start(bf16[8,128,512]{1,2,0:T(8,128)(2,1)} %bitcast.33), calls=%async_computation | async-start | bytes 2097152 | tf_op jit(solution)/shard_map/all_to_all | solution.py:16
  54.1 43.8 %copy-start = (bf16[128,4096]{1,0:T(8,128)(2,1)}, bf16[128,4096]{1,0:T(8,128)(2,1)S(1)}, u32[]{:S(2)}) copy-start(bf16[128,4096]{1,0:T(8,128)(2,1)S(1)} %collective-permute-done) | copy-start | bytes 3145732
  55.1 51.7 %collective-permute-start.1 = (bf16[64,4096]{1,0:T(8,128)(2,1)}, bf16[64,4096]{1,0:T(8,128)(2,1)}, u32[]{:S(2)}, u32[]{:S(2)}) collective-permute-start(bf16[64,4096]{1,0:T(8,128)(2,1)} %slice.18), channel_id=1, source_target_pairs={{0,38},{2,0},{4,2},{6,4},{32,6},{34,32},{36,34},{38,36},{1,39},{3,... | collective-permute-start | bytes 1572872 | tf_op jit(solution)/shard_map/ppermute | solution.py:12
  59.1 49.5 %collective-permute-start.3 = (bf16[64,4096]{1,0:T(8,128)(2,1)}, bf16[64,4096]{1,0:T(8,128)(2,1)}, u32[]{:S(2)}, u32[]{:S(2)}) collective-permute-start(bf16[64,4096]{1,0:T(8,128)(2,1)} %slice.19), channel_id=1, source_target_pairs={{0,2},{2,4},{4,6},{6,32},{32,34},{34,36},{36,38},{38,0},{1,3},{3,5... | collective-permute-start | bytes 1572872 | tf_op jit(solution)/shard_map/ppermute | solution.py:12
  99.6 30.1 %all-to-all-start.5 = ((bf16[4,4,32,2048]{3,2,1,0:T(8,128)(2,1)}), bf16[4,4,32,2048]{3,2,1,0:T(8,128)(2,1)S(1)}, u32[]{:S(2)}, u32[]{:S(2)}) async-start(bf16[4,4,32,2048]{3,2,1,0:T(8,128)(2,1)} %bitcast.31), calls=%async_computation.5 | async-start | bytes 4194304 | tf_op jit(solution)/shard_map/all_to_all | solution.py:16
  129.7 30.4 %all-to-all-start.2 = ((bf16[4,4,32,2048]{3,2,1,0:T(8,128)(2,1)}), bf16[4,4,32,2048]{3,2,1,0:T(8,128)(2,1)}, u32[]{:S(2)}, u32[]{:S(2)}) async-start(bf16[4,4,32,2048]{3,2,1,0:T(8,128)(2,1)} %bitcast.32), calls=%async_computation.2 | async-start | bytes 4194304 | tf_op jit(solution)/shard_map/all_to_all | solution.py:16
  160.1 17.7 %all-to-all-start.6 = ((bf16[4,32,2048]{2,1,0:T(8,128)(2,1)}), bf16[4,32,2048]{2,1,0:T(8,128)(2,1)S(1)}, u32[]{:S(2)}, u32[]{:S(2)}) async-start(bf16[4,32,2048]{2,1,0:T(8,128)(2,1)} %reduce_sum.50), calls=%async_computation.6 | async-start | bytes 1048576 | tf_op jit(solution)/shard_map/all_to_all | solution.py:16
  177.8 16.4 %all-to-all-start.3 = ((bf16[4,32,2048]{2,1,0:T(8,128)(2,1)}), bf16[4,32,2048]{2,1,0:T(8,128)(2,1)S(1)}, u32[]{:S(2)}, u32[]{:S(2)}) async-start(bf16[4,32,2048]{2,1,0:T(8,128)(2,1)} %reduce_sum.48), calls=%async_computation.3 | async-start | bytes 1048576 | tf_op jit(solution)/shard_map/all_to_all | solution.py:16
  194.2 38.2 %all-to-all-start.1 = ((bf16[4,1024,128]{1,2,0:T(8,128)(2,1)}), bf16[4,1024,128]{1,2,0:T(8,128)(2,1)S(1)}, u32[]{:S(2)}, u32[]{:S(2)}) async-start(bf16[4,1024,128]{1,2,0:T(8,128)(2,1)} %bitcast.9), calls=%async_computation.1 | async-start | bytes 2097152 | tf_op jit(solution)/shard_map/all_to_all | solution.py:16
  197.8 30.8 %collective-permute-start.5 = (bf16[32,2048]{1,0:T(8,128)(2,1)S(1)}, bf16[32,2048]{1,0:T(8,128)(2,1)S(1)}, u32[]{:S(2)}, u32[]{:S(2)}) collective-permute-start(bf16[32,2048]{1,0:T(8,128)(2,1)S(1)} %reduce_sum.51), channel_id=1, source_target_pairs={{0,32},{32,0},{1,33},{33,1},{2,34},{34,2},{3,35},{35,3},{4,36},{36... | collective-permute-start | bytes 393224 | tf_op jit(solution)/shard_map/ppermute | solution.py:12
  203.0 35.1 %collective-permute-start.4 = (bf16[32,2048]{1,0:T(8,128)(2,1)S(1)}, bf16[32,2048]{1,0:T(8,128)(2,1)S(1)}, u32[]{:S(2)}, u32[]{:S(2)}) collective-permute-start(bf16[32,2048]{1,0:T(8,128)(2,1)S(1)} %reduce_sum.49), channel_id=1, source_target_pairs={{0,32},{32,0},{1,33},{33,1},{2,34},{34,2},{3,35},{35,3},{4,36},{36... | collective-permute-start | bytes 393224 | tf_op jit(solution)/shard_map/ppermute | solution.py:12
  233.2 12.4 %all-to-all-start.7 = ((bf16[4,32,2048]{2,1,0:T(8,128)(2,1)}), bf16[4,32,2048]{2,1,0:T(8,128)(2,1)S(1)}, u32[]{:S(2)}, u32[]{:S(2)}) async-start(bf16[4,32,2048]{2,1,0:T(8,128)(2,1)} %broadcast_in_dim.5), calls=%async_computation.7 | async-start | bytes 1048576 | tf_op jit(solution)/shard_map/all_to_all | solution.py:16
  246.5 11.5 %all-to-all-start.4 = ((bf16[4,32,2048]{2,1,0:T(8,128)(2,1)}), bf16[4,32,2048]{2,1,0:T(8,128)(2,1)S(1)}, u32[]{:S(2)}, u32[]{:S(2)}) async-start(bf16[4,32,2048]{2,1,0:T(8,128)(2,1)} %broadcast_in_dim.4), calls=%async_computation.4 | async-start | bytes 1048576 | tf_op jit(solution)/shard_map/all_to_all | solution.py:16
Sparse Core Ops, SparseCore 0:
  9.9 48.8 all-gather.2
  60.6 32.7 all-gather.4
where the time goes:
time: 267 us; the launch traced here: 266 us
  waiting for transfers between devices  129 us (48%)
  starting transfers between devices  52.7 us (20%)
  local copies, waits for them, and re-layouts  36.6 us (14%)
  matrix products  20.5 us (8%)
  between operations  14.1 us (5%)
  other arithmetic  13.3 us (5%)
    all_to_all x8, waiting for transfers between devices, exchange(): return lax.all_to_all(v, axis, split_axis=0, concat_axis=0, tiled=True)  74.8 us
    all_to_all x8, starting transfers between devices, exchange(): return lax.all_to_all(v, axis, split_axis=0, concat_axis=0, tiled=True)  37.4 us
    all_gather x2, waiting for transfers between devices, local(): lax.all_gather(g[:, lo:hi], ('y', 'c'), axis=0, tiled=True)  28.4 us
    ppermute x6, waiting for transfers between devices, shift(): return lax.ppermute(v, axis, [(i, (i + by) % n) for i in range(n)])  24.7 us
    unnamed x14, local copies, waits for them, and re-layouts  18.8 us
    ppermute x6, starting transfers between devices, shift(): return lax.ppermute(v, axis, [(i, (i + by) % n) for i in range(n)])  15.3 us
    dot_general x2, matrix products, local(): lax.dot_general(acts, gj, (((0,), (0,)), ((), ())), preferred_element_typ...  10.5 us
    dot_general x1, matrix products, local(): lax.dot_general(gall, w, (((1,), (1,)), ((), ())), preferred_element_type...  10.1 us
  transfers between devices with their start and end apart: 16, of which 10 were waited for; matrix products, arithmetic and copies ran while one was open for 25% of the time, Pallas kernels for 0%

commit v1 on v0

--- a/solution.py
+++ b/solution.py
@@ -42,7 +42,15 @@
         size = size * feats // sum(CHUNKS)
         cuts.append((at, at + size))
         at += size
-    g_cols = [lax.all_gather(g[:, lo:hi], ("y", "c"), axis=0, tiled=True) for lo, hi in cuts]
+    g_cols = [
+        jnp.concatenate(
+            lax.all_to_all(
+                jnp.stack(lax.psum(1, ("y", "c")) * [g[:, lo:hi]], axis=0), ("y", "c"), 0, 0
+            ),
+            axis=0,
+        )
+        for lo, hi in cuts
+    ]
     a = a.reshape(toks, 4, 4, 2, heads).transpose(1, 3, 0, 2, 4).reshape(8, toks, 4 * heads)
     acts = exchange(a, ("y", "c")).reshape(8 * toks, 4 * heads)
     w_parts = around(w_out, RING8)

time: 267 us -> 302 us (1.13)
  blocking collectives: 0 us -> 53.6 us
  waiting for transfers between devices: 129 us -> 114 us
  between operations: 14.1 us -> 0.73 us
  starting transfers between devices: 52.7 us -> 58.9 us
    all_to_all x0 -> x1, blocking collectives: none -> 53.6 us  [local(): lax.all_to_all(jnp.stack(lax.psum(1, ('y', 'c')) * [g[:, lo:hi]], axis=0)...]
    all_gather x2 -> x0, waiting for transfers between devices: 28.4 us -> none  [local(): lax.all_gather(g[:, lo:hi], ('y', 'c'), axis=0, tiled=True)]
    ppermute x6, waiting for transfers between devices: 24.7 us -> 43.3 us  [shift(): return lax.ppermute(v, axis, [(i, (i + by) % n) for i in range(n)])]
    all_to_all x8, waiting for transfers between devices: 74.8 us -> 62.1 us  [exchange(): return lax.all_to_all(v, axis, split_axis=0, concat_axis=0, tiled=True)]
    all_to_all x0 -> x1, waiting for transfers between devices: none -> 9.17 us  [local(): lax.all_to_all(jnp.stack(lax.psum(1, ('y', 'c')) * [g[:, lo:hi]], axis=0)...]
    another operation x0 -> x4, local copies, waits for them, and re-layouts: none -> 6.95 us  [the longest x2 3.88 us: local(): a.reshape(toks, 4, 4, 2, heads).transpose(1, 3, 0, 2, 4)]
    all_to_all x0 -> x1, starting transfers between devices: none -> 4.55 us  [local(): lax.all_to_all(jnp.stack(lax.psum(1, ('y', 'c')) * [g[:, lo:hi]], axis=0)...]
    unnamed x14 -> x17, local copies, waits for them, and re-layouts: 18.8 us -> 16.6 us
  transfers between devices with their start and end apart: 16 -> 15, of which waited for: 10 -> 11; matrix products, arithmetic and copies ran while one was open for 25% -> 21% of each run, Pallas kernels for 0% -> 0%
where the time goes in v1:
time: 302 us; the launch traced here: 301 us
  waiting for transfers between devices  114 us (38%)
  starting transfers between devices  58.9 us (20%)
  blocking collectives  53.6 us (18%)
  local copies, waits for them, and re-layouts  38.7 us (13%)
  matrix products  20.8 us (7%)
  other arithmetic  13.3 us (4%)
    all_to_all x8, waiting for transfers between devices, exchange(): return lax.all_to_all(v, axis, split_axis=0, concat_axis=0, tiled=True)  62.1 us
    all_to_all x1, blocking collectives, local(): lax.all_to_all(jnp.stack(lax.psum(1, ('y', 'c')) * [g[:, lo:hi]], axis=0)...  53.6 us
    ppermute x6, waiting for transfers between devices, shift(): return lax.ppermute(v, axis, [(i, (i + by) % n) for i in range(n)])  43.3 us
    all_to_all x8, starting transfers between devices, exchange(): return lax.all_to_all(v, axis, split_axis=0, concat_axis=0, tiled=True)  38.6 us
    unnamed x17, local copies, waits for them, and re-layouts  16.6 us
    ppermute x6, starting transfers between devices, shift(): return lax.ppermute(v, axis, [(i, (i + by) % n) for i in range(n)])  15.7 us
    dot_general x2, matrix products, local(): lax.dot_general(acts, gj, (((0,), (0,)), ((), ())), preferred_element_typ...  10.8 us
    dot_general x1, matrix products, local(): lax.dot_general(gall, w, (((1,), (1,)), ((), ())), preferred_element_type...  10.1 us
  transfers between devices with their start and end apart: 15, of which 11 were waited for; matrix products, arithmetic and copies ran while one was open for 21% of the time, Pallas kernels for 0%

profile of v1, /device:TPU:2, one launch (start us, length us, event | category | flops | bytes accessed | tf_op | source)
XLA Modules:
  0.0 300.6 jit_solution(6989669576942418693)
XLA Ops:
  4.5 4.5 %all-to-all-start.2 = ((bf16[8,128,512]{1,2,0:T(8,128)(2,1)}), bf16[8,128,512]{1,2,0:T(8,128)(2,1)S(1)}, u32[]{:S(2)}, u32[]{:S(2)}) async-start(bf16[8,128,512]{1,2,0:T(8,128)(2,1)} %bitcast.4), calls=%async_computation.2 | async-start | bytes 2097152 | tf_op jit(solution)/shard_map/all_to_all | solution.py:16
  10.3 14.7 %all-to-all-done.2 = bf16[8,128,512]{1,2,0:T(8,128)(2,1)S(1)} async-done(((bf16[8,128,512]{1,2,0:T(8,128)(2,1)}), bf16[8,128,512]{1,2,0:T(8,128)(2,1)S(1)}, u32[]{:S(2)}, u32[]{:S(2)}) %all-to-all-start.2) | async-done | bytes 1048608 | tf_op jit(solution)/shard_map/all_to_all | solution.py:16
  25.5 53.6 %all_to_all.50 = bf16[8,128,2048]{2,1,0:T(8,128)(2,1)} all-to-all(bf16[8,128,2048]{2,1,0:T(8,128)(2,1)S(1)} %stack.4), channel_id=1, replica_groups=mesh['x'=4,'h'=2,'y'=4,'l'=4,'c'=2] {'y','c'}, dimensions={0} | all-to-all | bytes 8388608 | tf_op jit(solution)/shard_map/all_to_all | solution.py:47
  81.6 4.5 %all-to-all-start.1 = ((bf16[8,128,2048]{2,1,0:T(8,128)(2,1)}), bf16[8,128,2048]{2,1,0:T(8,128)(2,1)}, u32[]{:S(2)}, u32[]{:S(2)}) async-start(bf16[8,128,2048]{2,1,0:T(8,128)(2,1)} %stack.5), calls=%async_computation.1 | async-start | bytes 8388608 | tf_op jit(solution)/shard_map/all_to_all | solution.py:47
  86.2 5.9 %collective-permute-start = (bf16[128,4096]{1,0:T(8,128)(2,1)S(1)}, bf16[128,4096]{1,0:T(8,128)(2,1)S(1)}, u32[]{:S(2)}, u32[]{:S(2)}) collective-permute-start(bf16[128,4096]{1,0:T(8,128)(2,1)S(1)} %copy-done.1), channel_id=1, source_target_pairs={{0,38},{2,0},{4,2},{6,4},{32,6},{34,32},{36,34},{38,36},{1,39},{3,... | collective-permute-start | bytes 3145736 | tf_op jit(solution)/shard_map/ppermute | solution.py:12
  95.5 19.5 %collective-permute-done = bf16[128,4096]{1,0:T(8,128)(2,1)S(1)} collective-permute-done((bf16[128,4096]{1,0:T(8,128)(2,1)S(1)}, bf16[128,4096]{1,0:T(8,128)(2,1)S(1)}, u32[]{:S(2)}, u32[]{:S(2)}) %collective-permute-start) | collective-permute-done | bytes 1048608 | tf_op jit(solution)/shard_map/ppermute | solution.py:12
  120.5 6.2 %bitcast_convert_fusion = bf16[512,2048]{1,0:T(8,128)(2,1)} fusion(bf16[8,128,512]{1,2,0:T(8,128)(2,1)} %copy-done.2, bf16[8,128,2048]{2,1,0:T(8,128)(2,1)} %all_to_all.50), kind=kOutput, calls=%fused_computation.1 | convolution fusion | flops 2148532224 | bytes 7340032 | tf_op jit(solution)/shard_map/dot_general | solution.py:61
  126.7 9.2 %all-to-all-done.1 = bf16[8,128,2048]{2,1,0:T(8,128)(2,1)} async-done(((bf16[8,128,2048]{2,1,0:T(8,128)(2,1)}), bf16[8,128,2048]{2,1,0:T(8,128)(2,1)}, u32[]{:S(2)}, u32[]{:S(2)}) %all-to-all-start.1) | async-done | bytes 4194336 | tf_op jit(solution)/shard_map/all_to_all | solution.py:47
  135.9 4.6 %convolution_convert_fusion = bf16[2048,512]{0,1:T(8,128)(2,1)S(1)} fusion(bf16[1024,2048]{1,0:T(8,128)(2,1)} %bitcast.2, bf16[1024,512]{1,0:T(8,128)(2,1)S(1)} %bitcast.42), kind=kOutput, calls=%fused_computation.4 | convolution fusion | flops 2148532224 | bytes 7340032 | tf_op jit(solution)/shard_map/dot_general | solution.py:61
  142.1 4.9 %all-to-all-start.7 = ((bf16[4,4,32,2048]{3,2,1,0:T(8,128)(2,1)}), bf16[4,4,32,2048]{3,2,1,0:T(8,128)(2,1)S(1)}, u32[]{:S(2)}, u32[]{:S(2)}) async-start(bf16[4,4,32,2048]{3,2,1,0:T(8,128)(2,1)} %bitcast.35), calls=%async_computation.7 | async-start | bytes 4194304 | tf_op jit(solution)/shard_map/all_to_all | solution.py:16
  157.3 14.6 %all-to-all-done.7 = bf16[4,4,32,2048]{3,2,1,0:T(8,128)(2,1)S(1)} async-done(((bf16[4,4,32,2048]{3,2,1,0:T(8,128)(2,1)}), bf16[4,4,32,2048]{3,2,1,0:T(8,128)(2,1)S(1)}, u32[]{:S(2)}, u32[]{:S(2)}) %all-to-all-start.7) | async-done | bytes 2097184 | tf_op jit(solution)/shard_map/all_to_all | solution.py:16
  171.9 5.9 %all-to-all-start.4 = ((bf16[4,4,32,2048]{3,2,1,0:T(8,128)(2,1)}), bf16[4,4,32,2048]{3,2,1,0:T(8,128)(2,1)}, u32[]{:S(2)}, u32[]{:S(2)}) async-start(bf16[4,4,32,2048]{3,2,1,0:T(8,128)(2,1)} %bitcast.36), calls=%async_computation.4 | async-start | bytes 4194304 | tf_op jit(solution)/shard_map/all_to_all | solution.py:16
  187.5 14.5 %all-to-all-done.4 = bf16[4,4,32,2048]{3,2,1,0:T(8,128)(2,1)} async-done(((bf16[4,4,32,2048]{3,2,1,0:T(8,128)(2,1)}), bf16[4,4,32,2048]{3,2,1,0:T(8,128)(2,1)}, u32[]{:S(2)}, u32[]{:S(2)}) %all-to-all-start.4) | async-done | bytes 2097184 | tf_op jit(solution)/shard_map/all_to_all | solution.py:16
  202.0 5.3 %all-to-all-start.8 = ((bf16[4,32,2048]{2,1,0:T(8,128)(2,1)}), bf16[4,32,2048]{2,1,0:T(8,128)(2,1)S(1)}, u32[]{:S(2)}, u32[]{:S(2)}) async-start(bf16[4,32,2048]{2,1,0:T(8,128)(2,1)} %reduce_sum.50), calls=%async_computation.8 | async-start | bytes 1048576 | tf_op jit(solution)/shard_map/all_to_all | solution.py:16
  208.4 7.8 %pad_maximum_fusion = bf16[1024,4096]{1,0:T(8,128)(2,1)} fusion(bf16[1024,2048]{1,0:T(8,128)(2,1)} %bitcast.2, bf16[1024,2048]{1,0:T(8,128)(2,1)} %bitcast.34), kind=kLoop, calls=%fused_computation | loop fusion | flops 16777216 | bytes 16777216 | tf_op jit(solution)/shard_map/concatenate | solution.py:72
  219.4 4.8 %all-to-all-start.5 = ((bf16[4,32,2048]{2,1,0:T(8,128)(2,1)}), bf16[4,32,2048]{2,1,0:T(8,128)(2,1)S(1)}, u32[]{:S(2)}, u32[]{:S(2)}) async-start(bf16[4,32,2048]{2,1,0:T(8,128)(2,1)} %reduce_sum.48), calls=%async_computation.5 | async-start | bytes 1048576 | tf_op jit(solution)/shard_map/all_to_all | solution.py:16
  224.2 10.1 %fusion.2 = bf16[1024,512]{0,1:T(8,128)(2,1)} fusion(bf16[1024,4096]{1,0:T(8,128)(2,1)} %pad_maximum_fusion, bf16[1024,4096]{1,0:T(8,128)(2,1)} %constant_dynamic-update-slice_fusion, s32[]{:T(128)S(6)} %select_n.3), kind=kOutput, calls=%fused_computation.7 | convolution fusion | flops 4295491584 | bytes 13631492 | tf_op jit(solution)/shard_map/dot_general | solution.py:73
  239.4 5.1 %collective-permute-start.5 = (bf16[32,2048]{1,0:T(8,128)(2,1)S(1)}, bf16[32,2048]{1,0:T(8,128)(2,1)S(1)}, u32[]{:S(2)}, u32[]{:S(2)}) collective-permute-start(bf16[32,2048]{1,0:T(8,128)(2,1)S(1)} %reduce_sum.51), channel_id=1, source_target_pairs={{0,32},{32,0},{1,33},{33,1},{2,34},{34,2},{3,35},{35,3},{4,36},{36... | collective-permute-start | bytes 393224 | tf_op jit(solution)/shard_map/ppermute | solution.py:12
  245.6 23.7 %collective-permute-done.5 = bf16[32,2048]{1,0:T(8,128)(2,1)S(1)} collective-permute-done((bf16[32,2048]{1,0:T(8,128)(2,1)S(1)}, bf16[32,2048]{1,0:T(8,128)(2,1)S(1)}, u32[]{:S(2)}, u32[]{:S(2)}) %collective-permute-start.5) | collective-permute-done | bytes 131104 | tf_op jit(solution)/shard_map/ppermute | solution.py:12
  269.4 4.5 %all-to-all-done.3 = bf16[4,1024,128]{1,2,0:T(8,128)(2,1)S(1)} async-done(((bf16[4,1024,128]{1,2,0:T(8,128)(2,1)}), bf16[4,1024,128]{1,2,0:T(8,128)(2,1)S(1)}, u32[]{:S(2)}, u32[]{:S(2)}) %all-to-all-start.3) | async-done | bytes 1048608 | tf_op jit(solution)/shard_map/all_to_all | solution.py:16
  274.8 4.9 %all-to-all-start.9 = ((bf16[4,32,2048]{2,1,0:T(8,128)(2,1)}), bf16[4,32,2048]{2,1,0:T(8,128)(2,1)S(1)}, u32[]{:S(2)}, u32[]{:S(2)}) async-start(bf16[4,32,2048]{2,1,0:T(8,128)(2,1)} %broadcast_in_dim.5), calls=%async_computation.9 | async-start | bytes 1048576 | tf_op jit(solution)/shard_map/all_to_all | solution.py:16
  279.7 7.5 %all-to-all-done.9 = bf16[4,32,2048]{2,1,0:T(8,128)(2,1)S(1)} async-done(((bf16[4,32,2048]{2,1,0:T(8,128)(2,1)}), bf16[4,32,2048]{2,1,0:T(8,128)(2,1)S(1)}, u32[]{:S(2)}, u32[]{:S(2)}) %all-to-all-start.9) | async-done | bytes 524320 | tf_op jit(solution)/shard_map/all_to_all | solution.py:16
  288.0 4.9 %all-to-all-start.6 = ((bf16[4,32,2048]{2,1,0:T(8,128)(2,1)}), bf16[4,32,2048]{2,1,0:T(8,128)(2,1)S(1)}, u32[]{:S(2)}, u32[]{:S(2)}) async-start(bf16[4,32,2048]{2,1,0:T(8,128)(2,1)} %broadcast_in_dim.4), calls=%async_computation.6 | async-start | bytes 1048576 | tf_op jit(solution)/shard_map/all_to_all | solution.py:16
  295.2 4.4 %all-to-all-done.6 = bf16[4,32,2048]{2,1,0:T(8,128)(2,1)S(1)} async-done(((bf16[4,32,2048]{2,1,0:T(8,128)(2,1)}), bf16[4,32,2048]{2,1,0:T(8,128)(2,1)S(1)}, u32[]{:S(2)}, u32[]{:S(2)}) %all-to-all-start.6) | async-done | bytes 524320 | tf_op jit(solution)/shard_map/all_to_all | solution.py:16
  (50 shorter events, 54.4 us)
Async XLA Ops:
  4.5 20.4 %all-to-all-start.2 = ((bf16[8,128,512]{1,2,0:T(8,128)(2,1)}), bf16[8,128,512]{1,2,0:T(8,128)(2,1)S(1)}, u32[]{:S(2)}, u32[]{:S(2)}) async-start(bf16[8,128,512]{1,2,0:T(8,128)(2,1)} %bitcast.4), calls=%async_computation.2 | async-start | bytes 2097152 | tf_op jit(solution)/shard_map/all_to_all | solution.py:16
  25.0 56.7 %copy-start.2 = (bf16[8,128,512]{1,2,0:T(8,128)(2,1)}, bf16[8,128,512]{1,2,0:T(8,128)(2,1)S(1)}, u32[]{:S(2)}) copy-start(bf16[8,128,512]{1,2,0:T(8,128)(2,1)S(1)} %all-to-all-done.2) | copy-start | bytes 3145732
  79.1 7.1 %copy-start.1 = (bf16[128,4096]{1,0:T(8,128)(2,1)S(1)}, bf16[128,4096]{1,0:T(8,128)(2,1)}, u32[]{:S(2)}) copy-start(bf16[128,4096]{1,0:T(8,128)(2,1)} %param.5) | copy-start | bytes 3145732
  81.6 54.2 %all-to-all-start.1 = ((bf16[8,128,2048]{2,1,0:T(8,128)(2,1)}), bf16[8,128,2048]{2,1,0:T(8,128)(2,1)}, u32[]{:S(2)}, u32[]{:S(2)}) async-start(bf16[8,128,2048]{2,1,0:T(8,128)(2,1)} %stack.5), calls=%async_computation.1 | async-start | bytes 8388608 | tf_op jit(solution)/shard_map/all_to_all | solution.py:47
  86.2 28.8 %collective-permute-start = (bf16[128,4096]{1,0:T(8,128)(2,1)S(1)}, bf16[128,4096]{1,0:T(8,128)(2,1)S(1)}, u32[]{:S(2)}, u32[]{:S(2)}) collective-permute-start(bf16[128,4096]{1,0:T(8,128)(2,1)S(1)} %copy-done.1), channel_id=1, source_target_pairs={{0,38},{2,0},{4,2},{6,4},{32,6},{34,32},{36,34},{38,36},{1,39},{3,... | collective-permute-start | bytes 3145736 | tf_op jit(solution)/shard_map/ppermute | solution.py:12
  92.1 27.5 %collective-permute-start.2 = (bf16[128,4096]{1,0:T(8,128)(2,1)S(1)}, bf16[128,4096]{1,0:T(8,128)(2,1)S(1)}, u32[]{:S(2)}, u32[]{:S(2)}) collective-permute-start(bf16[128,4096]{1,0:T(8,128)(2,1)S(1)} %copy-done.1), channel_id=1, source_target_pairs={{0,2},{2,4},{4,6},{6,32},{32,34},{34,36},{36,38},{38,0},{1,3},{3,5... | collective-permute-start | bytes 3145736 | tf_op jit(solution)/shard_map/ppermute | solution.py:12
  115.0 25.4 %copy-start = (bf16[128,4096]{1,0:T(8,128)(2,1)}, bf16[128,4096]{1,0:T(8,128)(2,1)S(1)}, u32[]{:S(2)}) copy-start(bf16[128,4096]{1,0:T(8,128)(2,1)S(1)} %collective-permute-done) | copy-start | bytes 3145732
  115.9 33.3 %collective-permute-start.1 = (bf16[64,4096]{1,0:T(8,128)(2,1)}, bf16[64,4096]{1,0:T(8,128)(2,1)}, u32[]{:S(2)}, u32[]{:S(2)}) collective-permute-start(bf16[64,4096]{1,0:T(8,128)(2,1)} %slice.18), channel_id=1, source_target_pairs={{0,38},{2,0},{4,2},{6,4},{32,6},{34,32},{36,34},{38,36},{1,39},{3,... | collective-permute-start | bytes 1572872 | tf_op jit(solution)/shard_map/ppermute | solution.py:12
  119.6 16.2 %copy-start.3 = (bf16[8,128,512]{2,1,0:T(8,128)(2,1)S(1)}, bf16[8,128,512]{2,1,0:T(8,128)(2,1)}, u32[]{:S(2)}) copy-start(bf16[8,128,512]{2,1,0:T(8,128)(2,1)} %copy.16) | copy-start | bytes 3145732
  120.5 30.7 %collective-permute-start.3 = (bf16[64,4096]{1,0:T(8,128)(2,1)}, bf16[64,4096]{1,0:T(8,128)(2,1)}, u32[]{:S(2)}, u32[]{:S(2)}) collective-permute-start(bf16[64,4096]{1,0:T(8,128)(2,1)} %slice.19), channel_id=1, source_target_pairs={{0,2},{2,4},{4,6},{6,32},{32,34},{34,36},{36,38},{38,0},{1,3},{3,5... | collective-permute-start | bytes 1572872 | tf_op jit(solution)/shard_map/ppermute | solution.py:12
  142.1 29.8 %all-to-all-start.7 = ((bf16[4,4,32,2048]{3,2,1,0:T(8,128)(2,1)}), bf16[4,4,32,2048]{3,2,1,0:T(8,128)(2,1)S(1)}, u32[]{:S(2)}, u32[]{:S(2)}) async-start(bf16[4,4,32,2048]{3,2,1,0:T(8,128)(2,1)} %bitcast.35), calls=%async_computation.7 | async-start | bytes 4194304 | tf_op jit(solution)/shard_map/all_to_all | solution.py:16
  171.9 30.1 %all-to-all-start.4 = ((bf16[4,4,32,2048]{3,2,1,0:T(8,128)(2,1)}), bf16[4,4,32,2048]{3,2,1,0:T(8,128)(2,1)}, u32[]{:S(2)}, u32[]{:S(2)}) async-start(bf16[4,4,32,2048]{3,2,1,0:T(8,128)(2,1)} %bitcast.36), calls=%async_computation.4 | async-start | bytes 4194304 | tf_op jit(solution)/shard_map/all_to_all | solution.py:16
  202.0 17.4 %all-to-all-start.8 = ((bf16[4,32,2048]{2,1,0:T(8,128)(2,1)}), bf16[4,32,2048]{2,1,0:T(8,128)(2,1)S(1)}, u32[]{:S(2)}, u32[]{:S(2)}) async-start(bf16[4,32,2048]{2,1,0:T(8,128)(2,1)} %reduce_sum.50), calls=%async_computation.8 | async-start | bytes 1048576 | tf_op jit(solution)/shard_map/all_to_all | solution.py:16
  219.4 16.4 %all-to-all-start.5 = ((bf16[4,32,2048]{2,1,0:T(8,128)(2,1)}), bf16[4,32,2048]{2,1,0:T(8,128)(2,1)S(1)}, u32[]{:S(2)}, u32[]{:S(2)}) async-start(bf16[4,32,2048]{2,1,0:T(8,128)(2,1)} %reduce_sum.48), calls=%async_computation.5 | async-start | bytes 1048576 | tf_op jit(solution)/shard_map/all_to_all | solution.py:16
  235.8 38.1 %all-to-all-start.3 = ((bf16[4,1024,128]{1,2,0:T(8,128)(2,1)}), bf16[4,1024,128]{1,2,0:T(8,128)(2,1)S(1)}, u32[]{:S(2)}, u32[]{:S(2)}) async-start(bf16[4,1024,128]{1,2,0:T(8,128)(2,1)} %bitcast.11), calls=%async_computation.3 | async-start | bytes 2097152 | tf_op jit(solution)/shard_map/all_to_all | solution.py:16
  239.4 29.9 %collective-permute-start.5 = (bf16[32,2048]{1,0:T(8,128)(2,1)S(1)}, bf16[32,2048]{1,0:T(8,128)(2,1)S(1)}, u32[]{:S(2)}, u32[]{:S(2)}) collective-permute-start(bf16[32,2048]{1,0:T(8,128)(2,1)S(1)} %reduce_sum.51), channel_id=1, source_target_pairs={{0,32},{32,0},{1,33},{33,1},{2,34},{34,2},{3,35},{35,3},{4,36},{36... | collective-permute-start | bytes 393224 | tf_op jit(solution)/shard_map/ppermute | solution.py:12
  244.6 35.1 %collective-permute-start.4 = (bf16[32,2048]{1,0:T(8,128)(2,1)S(1)}, bf16[32,2048]{1,0:T(8,128)(2,1)S(1)}, u32[]{:S(2)}, u32[]{:S(2)}) collective-permute-start(bf16[32,2048]{1,0:T(8,128)(2,1)S(1)} %reduce_sum.49), channel_id=1, source_target_pairs={{0,32},{32,0},{1,33},{33,1},{2,34},{34,2},{3,35},{35,3},{4,36},{36... | collective-permute-start | bytes 393224 | tf_op jit(solution)/shard_map/ppermute | solution.py:12
  274.8 12.4 %all-to-all-start.9 = ((bf16[4,32,2048]{2,1,0:T(8,128)(2,1)}), bf16[4,32,2048]{2,1,0:T(8,128)(2,1)S(1)}, u32[]{:S(2)}, u32[]{:S(2)}) async-start(bf16[4,32,2048]{2,1,0:T(8,128)(2,1)} %broadcast_in_dim.5), calls=%async_computation.9 | async-start | bytes 1048576 | tf_op jit(solution)/shard_map/all_to_all | solution.py:16
  288.0 11.5 %all-to-all-start.6 = ((bf16[4,32,2048]{2,1,0:T(8,128)(2,1)}), bf16[4,32,2048]{2,1,0:T(8,128)(2,1)S(1)}, u32[]{:S(2)}, u32[]{:S(2)}) async-start(bf16[4,32,2048]{2,1,0:T(8,128)(2,1)} %broadcast_in_dim.4), calls=%async_computation.6 | async-start | bytes 1048576 | tf_op jit(solution)/shard_map/all_to_all | solution.py:16
